TPU v7x, 32 devices: a whole 2x2x4 slice. The times are simulated.
32 devices in a mesh: row: 8 (over y, x, core), col: 4 (over z).
Axes of the slice: x: 2, y: 2, z: 4, core: 2. Of those that a mesh axis runs over, the one named last changes fastest.
Arguments:
- tokens: bfloat16 [128, 96, 768], P('row', 'col'), as said below
- dw_kernel: float32 [7, 7, 768], replicated, may hold values from -0.875 to 0.875
- norm_gain: float32 [768], replicated, may hold values from 0.5 to 1.5
- norm_shift: float32 [768], replicated, may hold values from -3 to 3
- w_in: bfloat16 [768, 3072], P(None, 'col'), may hold values from -0.21875 to 0.21875
- w_out: bfloat16 [3072, 768], P('col'), may hold values from -0.109375 to 0.109375
- w_kv: bfloat16 [768, 1536], P(None, 'col'), as said below
- queries: bfloat16 [512, 768], replicated, may hold values from -300 to 300, as said below
- latent_gain: float32 [768], replicated, may hold values from 0.5 to 1.5
- w_o: bfloat16 [768, 768], P(None, 'col'), may hold values from -0.21875 to 0.21875
Outputs:
- token_map: bfloat16 [128, 96, 768], P('row', 'col')
- latents: bfloat16 [512, 768], replicated
Inputs may be any that keep to these rules, and one draw needn't show every extreme that they name: Latent queries; a few rows may be far larger than the others. `tokens`: patch token features, roughly unit normal, between -24 and 24; a few cells hold 24 in two channels. `w_kv`: key and value projection weights.
All inputs are finite; a program needn't handle non-finite values.
Results may differ from a plain program's by a relative error of at most 0.011.
Values may be sent and summed in bfloat16 or wider, within the bound.
A program may use at most 64 MiB of HBM per device.

v0:
```python
import math
import jax
import jax.numpy as jnp
from jax import lax
from jax.sharding import PartitionSpec as P

HEADS = 12
HEAD = 64


def with_halo(cells, sides, width):
    for axis, dim in sides:
        count = lax.axis_size(axis)
        ends = count - 1
        head = lax.slice_in_dim(cells, 0, width, axis=dim)
        tail = lax.slice_in_dim(cells, cells.shape[dim] - width, cells.shape[dim], axis=dim)
        cells = jnp.concatenate(
            [
                lax.ppermute(tail, axis, [(i, (i + 1) % count) for i in range(ends)]),
                cells,
                lax.ppermute(head, axis, [((i + 1) % count, i) for i in range(ends)]),
            ],
            axis=dim,
        )
    return cells


def conv_taps(padded, height, width, dw_kernel):
    mixed = jnp.zeros((height, width, padded.shape[2]), jnp.float32)
    for row_tap in range(7):
        for col_tap in range(7):
            mixed = (
                mixed
                + padded[row_tap : row_tap + height, col_tap : col_tap + width]
                * dw_kernel[row_tap, col_tap]
            )
    return mixed


def layer_norm(mixed, norm_gain, norm_shift):
    center = mixed - jnp.mean(mixed, axis=-1, keepdims=True)
    spread = jnp.mean(center * center, axis=-1, keepdims=True)
    return (center * lax.rsqrt(spread + 1e-06) * norm_gain + norm_shift).astype(jnp.bfloat16)


def finish_latents(numer, denom, latent_gain, w_full):
    attended = (numer / denom[..., None]).reshape(numer.shape[0], -1)
    squares = jnp.mean(attended * attended, axis=-1, keepdims=True)
    scaled = (attended * lax.rsqrt(squares + 1e-06) * latent_gain).astype(jnp.bfloat16)
    return jnp.dot(scaled, w_full, preferred_element_type=jnp.float32).astype(jnp.bfloat16)


def body(tokens, dw_kernel, norm_gain, norm_shift, w_in, w_out, w_kv, queries, latent_gain, w_o):
    height, width, width_d = tokens.shape
    latent_count = queries.shape[0]
    padded = with_halo(tokens, (("row", 0), ("col", 1)), 3)
    mixed = conv_taps(padded.astype(jnp.float32), height, width, dw_kernel)
    normed = layer_norm(mixed, norm_gain, norm_shift).reshape(height * width, width_d)
    residual = tokens.reshape(height * width, width_d).astype(jnp.float32)
    hidden = jax.nn.gelu(
        jnp.dot(
            normed,
            lax.all_gather(w_in, "col", axis=1, tiled=True),
            preferred_element_type=jnp.float32,
        )
    ).astype(jnp.bfloat16)
    update = jnp.dot(
        hidden, lax.all_gather(w_out, "col", axis=0, tiled=True), preferred_element_type=jnp.float32
    )
    token_rows = (residual + update).astype(jnp.bfloat16)
    token_map = token_rows.reshape(height, width, width_d)
    keys_vals = jnp.dot(
        token_rows,
        lax.all_gather(w_kv, "col", axis=1, tiled=True),
        preferred_element_type=jnp.float32,
    ).astype(jnp.bfloat16)
    w_full = lax.all_gather(w_o, "col", axis=1, tiled=True)
    key_heads = keys_vals[:, :width_d].reshape(-1, HEADS, HEAD)
    val_heads = keys_vals[:, width_d:].reshape(-1, HEADS, HEAD)
    query_heads = queries.reshape(latent_count, HEADS, HEAD)
    score_scale = 1.0 / math.sqrt(HEAD)
    group_size = math.gcd(HEADS, 4)
    max_parts, den_parts, num_parts = ([], [], [])
    for first_head in range(0, HEADS, group_size):
        scores = (
            jnp.einsum(
                "lhd,thd->lht",
                query_heads[:, first_head : first_head + group_size],
                key_heads[:, first_head : first_head + group_size],
                preferred_element_type=jnp.float32,
            )
            * score_scale
        )
        local_max = jnp.max(scores, axis=-1)
        weights = jnp.exp(scores - local_max[..., None])
        den_parts.append(jnp.sum(weights, axis=-1))
        max_parts.append(local_max)
        num_parts.append(
            jnp.einsum(
                "lht,thd->lhd",
                weights.astype(jnp.bfloat16),
                val_heads[:, first_head : first_head + group_size],
                preferred_element_type=jnp.float32,
            )
        )
    maxima = jnp.concatenate(max_parts, axis=1)
    denom = jnp.concatenate(den_parts, axis=1)
    numer = jnp.concatenate(num_parts, axis=1)
    peak = lax.pmax(maxima, ("row", "col"))
    factor = jnp.exp(maxima - peak)
    den_terms = denom * factor
    num_terms = (numer * factor[..., None]).reshape(latent_count, width_d)
    den_part, num_part = (
        lax.psum_scatter(den_terms, "col", scatter_dimension=0, tiled=True),
        lax.psum_scatter(num_terms, "col", scatter_dimension=0, tiled=True),
    )
    den_share, num_share = lax.psum((den_part, num_part), "row")
    own_rows = finish_latents(
        num_share.reshape(num_share.shape[0], HEADS, HEAD), den_share, latent_gain, w_full
    )
    latents = lax.all_gather(own_rows, "col", axis=0, tiled=True)
    return (token_map, latents)


def solution(mesh):
    in_specs = (
        P("row", "col", None),
        P(),
        P(),
        P(),
        P(None, "col"),
        P("col", None),
        P(None, "col"),
        P(),
        P(),
        P(None, "col"),
    )
    out_specs = (P("row", "col", None), P())
    return jax.shard_map(body, mesh=mesh, in_specs=in_specs, out_specs=out_specs, check_vma=False)
```

profile of v0, /device:TPU:0, one launch (start us, length us, event | category | flops | bytes accessed | tf_op | source)
XLA Modules:
  0.0 479.7 jit_solution(5248755326156885472)
XLA Ops:
  7.2 0.7 all-gather.5.cloned.1.call-update
  8.0 0.7 all-gather.7.cloned.1.call-update
  8.8 2.4 collective-permute-start
  11.2 1.3 collective-permute-start.1
  12.6 0.2 slice_reduce_fusion.47
  12.7 1.2 copy.24
  13.9 0.2 slice_reduce_fusion.48
  14.1 2.3 collective-permute-done.1
  16.5 0.1 fusion.112
  16.6 3.5 collective-permute-start.2
  20.1 1.3 collective-permute-start.3
  21.5 4.3 collective-permute-done.2
  25.8 7.4 %collective-permute-done.3 = bf16[22,3,768]{2,1,0:T(4,128)(2,1)S(1)} collective-permute-done((bf16[22,3,768]{2,1,0:T(4,128)(2,1)S(1)}, bf16[22,3,768]{2,1,0:T(4,128)(2,1)S(1)}, u32[]{:S(2)}, u32[]{:S(2)}) %collective-permute-start.3) | collective-permute-done | bytes 101408 | tf_op jit(solution)/shard_map/ppermute | solution.py:21
  33.2 0.4 maximum_convert_fusion
  33.6 12.3 %fusion.109 = (f32[16,24]{1,0:T(8,128)S(1)}, f32[16,24,768]{2,1,0:T(8,128)S(1)}) fusion(f32[768]{0:T(1024)S(1)} %get-tuple-element.49, f32[22,30,768]{2,1,0:T(8,128)S(1)} %maximum_convert_fusion, f32[768]{0:T(1024)S(1)} %get-tuple-element.50, f32[768]{0:T(1024)S(1)} %get-tuple-element.3, f32[768]{0:T(1024)S(1)} %get-tuple-element.4, ...), kind=kLoop, calls=%fused_computation.218 | loop fusion | flops 28900992 | bytes 59134464 | tf_op jit(solution)/shard_map/reduce_sum | solution.py:41
  45.9 0.3 multiply_reduce_fusion
  46.2 0.4 copy-done.7
  46.6 0.3 add_convert_fusion
  46.8 57.7 %all-gather.5.cloned.1.call-done = bf16[768,3072]{1,0:T(8,128)(2,1)} async-done(((bf16[768,768]{1,0:T(8,128)(2,1)}), bf16[768,3072]{1,0:T(8,128)(2,1)}) %all-gather.5.cloned.1.call-update) | async-done | bytes 4718608 | tf_op jit(solution)/shard_map/all_gather | solution.py:63
  104.6 89.4 %all-gather.7.cloned.1.call-done = bf16[3072,768]{1,0:T(8,128)(2,1)} async-done(((bf16[768,768]{1,0:T(8,128)(2,1)}), bf16[3072,768]{1,0:T(8,128)(2,1)}) %all-gather.7.cloned.1.call-update) | async-done | bytes 4718608 | tf_op jit(solution)/shard_map/all_gather | solution.py:68
  193.9 7.9 %fusion.34 = bf16[384,768]{1,0:T(8,128)(2,1)S(1)} fusion(bf16[3072,768]{1,0:T(8,128)(2,1)} %all-gather.7.cloned.1.call-done, bf16[384,768]{1,0:T(8,128)(2,1)S(1)} %bitcast.66, bf16[384,768]{1,0:T(8,128)(2,1)S(1)} %bitcast.70, bf16[768,3072]{1,0:T(8,128)(2,1)} %all-gather.5.cloned.1.call-done), kind=kOutput, calls=%fused_computation.37 | convolution fusion | flops 3635380224 | bytes 11206656 | tf_op jit(solution)/shard_map/dot_general | solution.py:67
  201.9 42.4 %all-gather.9.cloned.1.call-done = bf16[768,1536]{1,0:T(8,128)(2,1)} async-done(((bf16[768,384]{1,0:T(8,128)(2,1)}), bf16[768,1536]{1,0:T(8,128)(2,1)}) %all-gather.9.cloned.1.call-update) | async-done | bytes 2359312 | tf_op jit(solution)/shard_map/all_gather | solution.py:74
  244.2 2.7 convolution_convert_fusion
  247.0 0.9 fusion.111
  247.9 1.0 copy.23
  248.9 1.8 bitcast_reduce_fusion
  250.8 2.3 bitcast_reduce_fusion.1
  253.0 2.3 bitcast_reduce_fusion.2
  255.4 2.1 copy.22
  257.5 3.6 fusion.37
  261.1 3.0 fusion.11
  264.1 1.5 fusion.40
  265.6 0.5 fusion.15
  266.2 1.5 fusion.43
  267.6 39.0 %pmax.7 = f32[512,12]{0,1:T(8,128)S(1)} all-reduce(f32[512,12]{0,1:T(8,128)S(1)} %pad_maximum_fusion), channel_id=1, replica_groups=mesh['row'=8,'col'=4] {'row','col'}, use_global_device_ids=true, to_apply=%region_5.0 | all-reduce | flops 6144 | bytes 49152 | tf_op jit(solution)/shard_map/pmax | solution.py:109
  306.7 0.6 maximum_multiply_fusion.1
  307.3 2.7 maximum_multiply_fusion
  310.0 0.5 reduce-scatter.5.cloned.1.call-update
  310.6 34.6 %reduce-scatter.3.cloned.1.call-done = f32[128,768]{0,1:T(8,128)} async-done(((f32[512,768]{0,1:T(8,128)}), f32[128,768]{0,1:T(8,128)}) %reduce-scatter.3.cloned.1.call-update) | async-done | bytes 393232 | tf_op jit(solution)/shard_map/reduce_scatter | solution.py:115
  345.3 0.7 all-gather.11.cloned.1.call-update
  346.0 19.4 %reduce-scatter.5.cloned.1.call-done = f32[128,12]{0,1:T(8,128)} async-done(((f32[512,12]{0,1:T(8,128)}), f32[128,12]{0,1:T(8,128)}) %reduce-scatter.5.cloned.1.call-update) | async-done | bytes 6160 | tf_op jit(solution)/shard_map/reduce_scatter | solution.py:114
  365.4 12.2 %psum.15 = f32[128,12]{0,1:T(8,128)S(1)} all-reduce(f32[128,12]{0,1:T(8,128)} %reduce-scatter.5.cloned.1.call-done), channel_id=1, replica_groups=mesh['row'=8,'col'=4] {'row'}, use_global_device_ids=true, to_apply=%region_12.0 | all-reduce | flops 1536 | bytes 12288 | tf_op jit(solution)/shard_map/psum | solution.py:117
  377.7 43.2 %all-reduce.2.cloned.1.call-done = f32[128,768]{0,1:T(8,128)} async-done(((f32[128,768]{0,1:T(8,128)}), f32[128,768]{0,1:T(8,128)}) %all-reduce.2.cloned.1.call-update) | async-done | bytes 393232 | tf_op jit(solution)/shard_map/psum | solution.py:117
  420.9 1.1 multiply_reduce_fusion.1
  422.0 30.1 %all-gather.11.cloned.1.call-done = bf16[768,768]{0,1:T(8,128)(2,1)} async-done(((bf16[768,192]{0,1:T(8,128)(2,1)}), bf16[768,768]{0,1:T(8,128)(2,1)}) %all-gather.11.cloned.1.call-update) | async-done | bytes 1179664 | tf_op jit(solution)/shard_map/all_gather | solution.py:77
  452.1 1.9 convolution_convert_fusion.1
  454.0 17.9 %all_gather.19 = bf16[512,768]{1,0:T(8,128)(2,1)S(1)} all-gather(bf16[128,768]{1,0:T(8,128)(2,1)S(1)} %convolution_convert_fusion.1), channel_id=1, replica_groups=mesh['row'=8,'col'=4] {'col'}, dimensions={0}, use_global_device_ids=true | all-gather | bytes 983040 | tf_op jit(solution)/shard_map/all_gather | solution.py:121
  471.9 0.9 copy.35
  (41 shorter events, 0.6 us)
Async XLA Ops:
  7.2 1.6 copy-start.1
  7.2 97.4 %all-gather.5.cloned.1.call-start = ((), (), s32[]{:S(2)}) async-start(), calls=%async_computation.2 | async-start | bytes 5898240 | tf_op jit(solution)/shard_map/all_gather | solution.py:63
  7.9 4.6 copy-start.6
  7.9 4.8 %copy-start.2 = (bf16[512,768]{1,0:T(8,128)(2,1)S(1)}, bf16[512,768]{1,0:T(8,128)(2,1)}, u32[]{:S(2)}) copy-start(bf16[512,768]{1,0:T(8,128)(2,1)} %param.17) | copy-start | bytes 2359300
  7.9 186.0 %all-gather.7.cloned.1.call-start = ((), (), s32[]{:S(2)}) async-start(), calls=%async_computation.3 | async-start | bytes 5898240 | tf_op jit(solution)/shard_map/all_gather | solution.py:68
  8.7 235.6 %all-gather.9.cloned.1.call-start = ((), (), s32[]{:S(2)}) async-start(), calls=%async_computation.4 | async-start | bytes 2949120 | tf_op jit(solution)/shard_map/all_gather | solution.py:74
  8.8 5.3 %collective-permute-start = (bf16[3,24,768]{2,1,0:T(8,128)(2,1)S(1)}, bf16[3,24,768]{2,1,0:T(8,128)(2,1)S(1)}, u32[]{:S(2)}, u32[]{:S(2)}) collective-permute-start(bf16[3,24,768]{2,1,0:T(8,128)(2,1)S(1)} %get-tuple-element.62), channel_id=1, source_target_pairs={{0,4},{4,8},{8,12},{12,16},{16,20},{20,24},{24,28},{1,5},{5,9},{9,... | collective-permute-start | bytes 331784 | tf_op jit(solution)/shard_map/ppermute | solution.py:19
  11.2 5.3 %collective-permute-start.1 = (bf16[3,24,768]{2,1,0:T(8,128)(2,1)S(1)}, bf16[3,24,768]{2,1,0:T(8,128)(2,1)S(1)}, u32[]{:S(2)}, u32[]{:S(2)}) collective-permute-start(bf16[3,24,768]{2,1,0:T(8,128)(2,1)S(1)} %get-tuple-element.61), channel_id=1, source_target_pairs={{4,0},{8,4},{12,8},{16,12},{20,16},{24,20},{28,24},{5,1},{9,5},{13... | collective-permute-start | bytes 331784 | tf_op jit(solution)/shard_map/ppermute | solution.py:21
  12.5 332.7 %reduce-scatter.3.cloned.1.call-start = ((), (), s32[]{:S(2)}) async-start(), calls=%async_computation.5 | async-start | bytes 1966080 | tf_op jit(solution)/shard_map/reduce_scatter | solution.py:115
  16.6 9.2 %collective-permute-start.2 = (bf16[22,3,768]{2,1,0:T(4,128)(2,1)S(1)}, bf16[22,3,768]{2,1,0:T(4,128)(2,1)S(1)}, u32[]{:S(2)}, u32[]{:S(2)}) collective-permute-start(bf16[22,3,768]{2,1,0:T(4,128)(2,1)S(1)} %get-tuple-element.59), channel_id=1, source_target_pairs={{0,1},{1,2},{2,3},{4,5},{5,6},{6,7},{8,9},{9,10},{10,11},{12,13},{... | collective-permute-start | bytes 304136 | tf_op jit(solution)/shard_map/ppermute | solution.py:19
  20.1 13.1 %collective-permute-start.3 = (bf16[22,3,768]{2,1,0:T(4,128)(2,1)S(1)}, bf16[22,3,768]{2,1,0:T(4,128)(2,1)S(1)}, u32[]{:S(2)}, u32[]{:S(2)}) collective-permute-start(bf16[22,3,768]{2,1,0:T(4,128)(2,1)S(1)} %get-tuple-element.60), channel_id=1, source_target_pairs={{1,0},{2,1},{3,2},{5,4},{6,5},{7,6},{9,8},{10,9},{11,10},{13,12},{... | collective-permute-start | bytes 304136 | tf_op jit(solution)/shard_map/ppermute | solution.py:21
  45.9 0.7 copy-start.7
  45.9 0.7 copy-start.8
  201.9 45.1 %copy-start.10 = (bf16[384,768]{1,0:T(8,128)(2,1)}, bf16[384,768]{1,0:T(8,128)(2,1)S(1)}, u32[]{:S(2)}) copy-start(bf16[384,768]{1,0:T(8,128)(2,1)S(1)} %fusion.34) | copy-start | bytes 1769476
  248.9 1.8 copy-start.3
  248.9 1.8 copy-start.5
  257.5 3.6 copy-start
  261.1 3.0 copy-start.4
  310.0 142.2 %copy-start.9 = (f32[768]{0:T(1024)S(1)}, f32[768]{0:T(1024)}, u32[]{:S(2)}) copy-start(f32[768]{0:T(1024)} %param.18) | copy-start | bytes 9220
  310.0 55.4 %reduce-scatter.5.cloned.1.call-start = ((), (), s32[]{:S(2)}) async-start(), calls=%async_computation.7 | async-start | bytes 40960 | tf_op jit(solution)/shard_map/reduce_scatter | solution.py:114
  310.6 110.3 %all-reduce.2.cloned.1.call-start = ((), (), s32[]{:S(2)}) async-start(), calls=%async_computation.6 | async-start | bytes 786432 | tf_op jit(solution)/shard_map/psum | solution.py:117
  345.2 106.9 %all-gather.11.cloned.1.call-start = ((), (), s32[]{:S(2)}) async-start(), calls=%async_computation.8 | async-start | bytes 1474560 | tf_op jit(solution)/shard_map/all_gather | solution.py:77
Sparse Core Ops, SparseCore 0:
  9.6 94.9 all-gather.4
  106.1 87.7 all-gather.6
  195.6 48.6 all-gather.8
  310.1 35.0 reduce-scatter.2
  347.3 18.0 reduce-scatter.4
  368.4 52.5 all-reduce.1
  422.5 29.6 all-gather.10
where the time goes:
time: 480 us
  waiting for transfers between devices  334 us (70%)
  blocking collectives  69.1 us (14%)
  matrix products  25.5 us (5%)
  other arithmetic  21.2 us (4%)
  between operations  14.4 us (3%)
  starting transfers between devices  8.75 us (2%)
  local copies, waits for them, and re-layouts  7.14 us (1%)
    all_gather x1, waiting for transfers between devices, body(): lax.all_gather(w_out, 'col', axis=0, tiled=True)  89.4 us
    all_gather x1, waiting for transfers between devices, body(): lax.all_gather(w_in, 'col', axis=1, tiled=True)  57.7 us
    psum x1, waiting for transfers between devices, body(): den_share, num_share = lax.psum((den_part, num_part), 'row')  43.2 us
    all_gather x1, waiting for transfers between devices, body(): lax.all_gather(w_kv, 'col', axis=1, tiled=True)  42.4 us
    pmax x1, blocking collectives, body(): peak = lax.pmax(maxima, ('row', 'col'))  39 us
    reduce_scatter x1, waiting for transfers between devices, body(): lax.psum_scatter(num_terms, 'col', scatter_dimension=0, tiled=True)  34.6 us
    all_gather x1, waiting for transfers between devices, body(): w_full = lax.all_gather(w_o, 'col', axis=1, tiled=True)  30.1 us
    reduce_scatter x1, waiting for transfers between devices, body(): lax.psum_scatter(den_terms, 'col', scatter_dimension=0, tiled=True)  19.4 us
  transfers between devices with their start and end apart: 11, of which 10 were waited for; matrix products, arithmetic and copies ran while one was open for 5% of the time, Pallas kernels for 0%

commit v1 on v0

--- a/solution.py
+++ b/solution.py
@@ -74,7 +74,12 @@
         lax.all_gather(w_kv, "col", axis=1, tiled=True),
         preferred_element_type=jnp.float32,
     ).astype(jnp.bfloat16)
-    w_full = lax.all_gather(w_o, "col", axis=1, tiled=True)
+    ring = [w_o]
+    for hop in range(3):
+        ring.append(lax.ppermute(ring[-1], "col", [(dev, (dev + 1) % 4) for dev in range(4)]))
+    w_full = jnp.roll(
+        jnp.concatenate(ring[::-1], axis=1), (lax.axis_index("col") + 1) * ring[0].shape[1], axis=1
+    )
     key_heads = keys_vals[:, :width_d].reshape(-1, HEADS, HEAD)
     val_heads = keys_vals[:, width_d:].reshape(-1, HEADS, HEAD)
     query_heads = queries.reshape(latent_count, HEADS, HEAD)

time: 480 us -> 465 us (0.969)
  waiting for transfers between devices: 334 us -> 309 us
  starting transfers between devices: 8.75 us -> 16.8 us
    ppermute x0 -> x3, waiting for transfers between devices: none -> 39.2 us  [body(): lax.ppermute(ring[-1], 'col', [(dev, (dev + 1) % 4) for dev in range(4)])]
    reduce_scatter x1, waiting for transfers between devices: 34.6 us -> 1.24 us  [body(): lax.psum_scatter(num_terms, 'col', scatter_dimension=0, tiled=True)]
    all_gather x1 -> x0, waiting for transfers between devices: 30.1 us -> none  [body(): w_full = lax.all_gather(w_o, 'col', axis=1, tiled=True)]
    ppermute x0 -> x3, starting transfers between devices: none -> 8.11 us  [body(): lax.ppermute(ring[-1], 'col', [(dev, (dev + 1) % 4) for dev in range(4)])]
  transfers between devices with their start and end apart: 11 -> 13, of which waited for: 10 -> 12; matrix products, arithmetic and copies ran while one was open for 5% -> 5% of each run, Pallas kernels for 0% -> 0%
where the time goes in v1:
time: 465 us
  waiting for transfers between devices  309 us (66%)
  blocking collectives  70.7 us (15%)
  matrix products  24.2 us (5%)
  other arithmetic  21.2 us (5%)
  starting transfers between devices  16.8 us (4%)
  between operations  14.5 us (3%)
  local copies, waits for them, and re-layouts  8.2 us (2%)
    all_gather x1, waiting for transfers between devices, body(): lax.all_gather(w_out, 'col', axis=0, tiled=True)  89.4 us
    all_gather x1, waiting for transfers between devices, body(): lax.all_gather(w_in, 'col', axis=1, tiled=True)  57.7 us
    psum x1, waiting for transfers between devices, body(): den_share, num_share = lax.psum((den_part, num_part), 'row')  43.3 us
    all_gather x1, waiting for transfers between devices, body(): lax.all_gather(w_kv, 'col', axis=1, tiled=True)  42.4 us
    ppermute x3, waiting for transfers between devices, body(): lax.ppermute(ring[-1], 'col', [(dev, (dev + 1) % 4) for dev in range(4)])  39.2 us
    pmax x1, blocking collectives, body(): peak = lax.pmax(maxima, ('row', 'col'))  39 us
    reduce_scatter x1, waiting for transfers between devices, body(): lax.psum_scatter(den_terms, 'col', scatter_dimension=0, tiled=True)  20.4 us
    all_gather x1, blocking collectives, body(): latents = lax.all_gather(own_rows, 'col', axis=0, tiled=True)  19.5 us
  transfers between devices with their start and end apart: 13, of which 12 were waited for; matrix products, arithmetic and copies ran while one was open for 5% of the time, Pallas kernels for 0%

profile of v1, /device:TPU:0, one launch (start us, length us, event | category | flops | bytes accessed | tf_op | source)
XLA Modules:
  0.0 464.7 jit_solution(15265887340997864318)
XLA Ops:
  7.2 0.7 all-gather.4.cloned.1.call-update
  8.0 0.7 all-gather.6.cloned.1.call-update
  8.8 2.4 collective-permute-start
  11.2 1.3 collective-permute-start.1
  12.7 1.2 copy.24
  14.1 2.3 collective-permute-done.1
  16.6 3.5 collective-permute-start.2
  20.1 1.3 collective-permute-start.3
  21.5 4.3 collective-permute-done.2
  25.8 7.4 %collective-permute-done.3 = bf16[22,3,768]{2,1,0:T(4,128)(2,1)S(1)} collective-permute-done((bf16[22,3,768]{2,1,0:T(4,128)(2,1)S(1)}, bf16[22,3,768]{2,1,0:T(4,128)(2,1)S(1)}, u32[]{:S(2)}, u32[]{:S(2)}) %collective-permute-start.3) | collective-permute-done | bytes 101408 | tf_op jit(solution)/shard_map/ppermute | solution.py:21
  33.2 0.4 maximum_convert_fusion
  33.6 12.3 %fusion.115 = (f32[16,24]{1,0:T(8,128)S(1)}, f32[16,24,768]{2,1,0:T(8,128)S(1)}) fusion(f32[768]{0:T(1024)S(1)} %get-tuple-element.49, f32[22,30,768]{2,1,0:T(8,128)S(1)} %maximum_convert_fusion, f32[768]{0:T(1024)S(1)} %get-tuple-element.50, f32[768]{0:T(1024)S(1)} %get-tuple-element.3, f32[768]{0:T(1024)S(1)} %get-tuple-element.4, ...), kind=kLoop, calls=%fused_computation.229 | loop fusion | flops 28900992 | bytes 59134464 | tf_op jit(solution)/shard_map/reduce_sum | solution.py:41
  45.9 0.3 multiply_reduce_fusion
  46.2 0.4 copy-done.8
  46.8 57.7 %all-gather.4.cloned.1.call-done = bf16[768,3072]{1,0:T(8,128)(2,1)} async-done(((bf16[768,768]{1,0:T(8,128)(2,1)}), bf16[768,3072]{1,0:T(8,128)(2,1)}) %all-gather.4.cloned.1.call-update) | async-done | bytes 4718608 | tf_op jit(solution)/shard_map/all_gather | solution.py:63
  104.6 89.4 %all-gather.6.cloned.1.call-done = bf16[3072,768]{1,0:T(8,128)(2,1)} async-done(((bf16[768,768]{1,0:T(8,128)(2,1)}), bf16[3072,768]{1,0:T(8,128)(2,1)}) %all-gather.6.cloned.1.call-update) | async-done | bytes 4718608 | tf_op jit(solution)/shard_map/all_gather | solution.py:68
  193.9 7.9 %fusion.34 = bf16[384,768]{1,0:T(8,128)(2,1)S(1)} fusion(bf16[3072,768]{1,0:T(8,128)(2,1)} %all-gather.6.cloned.1.call-done, bf16[384,768]{1,0:T(8,128)(2,1)S(1)} %bitcast.65, bf16[384,768]{1,0:T(8,128)(2,1)S(1)} %bitcast.69, bf16[768,3072]{1,0:T(8,128)(2,1)} %all-gather.4.cloned.1.call-done), kind=kOutput, calls=%fused_computation.37 | convolution fusion | flops 3635380224 | bytes 11206656 | tf_op jit(solution)/shard_map/dot_general | solution.py:67
  201.9 42.4 %all-gather.8.cloned.1.call-done = bf16[768,1536]{1,0:T(8,128)(2,1)} async-done(((bf16[768,384]{1,0:T(8,128)(2,1)}), bf16[768,1536]{1,0:T(8,128)(2,1)}) %all-gather.8.cloned.1.call-update) | async-done | bytes 2359312 | tf_op jit(solution)/shard_map/all_gather | solution.py:74
  244.2 2.7 convolution_convert_fusion
  247.0 0.9 fusion.117
  247.9 1.0 copy.23
  248.9 1.8 bitcast_reduce_fusion
  250.8 2.3 bitcast_reduce_fusion.1
  253.0 2.3 bitcast_reduce_fusion.2
  255.4 2.1 copy.22
  257.5 3.6 fusion.37
  261.1 3.0 fusion.11
  264.1 1.5 fusion.40
  265.6 0.5 fusion.15
  266.2 1.5 fusion.43
  267.6 39.0 %pmax.7 = f32[512,12]{0,1:T(8,128)S(1)} all-reduce(f32[512,12]{0,1:T(8,128)S(1)} %pad_maximum_fusion), channel_id=1, replica_groups=mesh['row'=8,'col'=4] {'row','col'}, use_global_device_ids=true, to_apply=%region_5.6 | all-reduce | flops 6144 | bytes 49152 | tf_op jit(solution)/shard_map/pmax | solution.py:114
  306.6 0.6 maximum_multiply_fusion.1
  307.3 2.7 maximum_multiply_fusion
  310.0 0.9 copy-done.1
  310.9 1.7 collective-permute-start.4
  312.6 10.9 %collective-permute-done.4 = bf16[768,192]{0,1:T(8,128)(2,1)S(1)} collective-permute-done((bf16[768,192]{0,1:T(8,128)(2,1)S(1)}, bf16[768,192]{0,1:T(8,128)(2,1)S(1)}, u32[]{:S(2)}, u32[]{:S(2)}) %collective-permute-start.4) | collective-permute-done | bytes 294944 | tf_op jit(solution)/shard_map/ppermute | solution.py:79
  323.5 2.5 collective-permute-start.5
  325.9 13.8 %collective-permute-done.5 = bf16[768,192]{0,1:T(8,128)(2,1)S(1)} collective-permute-done((bf16[768,192]{0,1:T(8,128)(2,1)S(1)}, bf16[768,192]{0,1:T(8,128)(2,1)S(1)}, u32[]{:S(2)}, u32[]{:S(2)}) %collective-permute-start.5) | collective-permute-done | bytes 294944 | tf_op jit(solution)/shard_map/ppermute | solution.py:79
  339.7 4.0 collective-permute-start.6
  343.7 14.6 %collective-permute-done.6 = bf16[768,192]{0,1:T(8,128)(2,1)S(1)} collective-permute-done((bf16[768,192]{0,1:T(8,128)(2,1)S(1)}, bf16[768,192]{0,1:T(8,128)(2,1)S(1)}, u32[]{:S(2)}, u32[]{:S(2)}) %collective-permute-start.6) | collective-permute-done | bytes 294944 | tf_op jit(solution)/shard_map/ppermute | solution.py:79
  358.5 1.2 reduce-scatter.3.cloned.1.call-done
  359.8 20.4 %reduce-scatter.5.cloned.1.call-done = f32[128,12]{0,1:T(8,128)} async-done(((f32[512,12]{0,1:T(8,128)}), f32[128,12]{0,1:T(8,128)}) %reduce-scatter.5.cloned.1.call-update) | async-done | bytes 6160 | tf_op jit(solution)/shard_map/reduce_scatter | solution.py:119
  380.2 12.2 %psum.15 = f32[128,12]{0,1:T(8,128)S(1)} all-reduce(f32[128,12]{0,1:T(8,128)} %reduce-scatter.5.cloned.1.call-done), channel_id=1, replica_groups=mesh['row'=8,'col'=4] {'row'}, use_global_device_ids=true, to_apply=%region_12.13 | all-reduce | flops 1536 | bytes 12288 | tf_op jit(solution)/shard_map/psum | solution.py:122
  392.4 43.3 %all-reduce.2.cloned.1.call-done = f32[128,768]{0,1:T(8,128)} async-done(((f32[128,768]{0,1:T(8,128)}), f32[128,768]{0,1:T(8,128)}) %all-reduce.2.cloned.1.call-update) | async-done | bytes 393232 | tf_op jit(solution)/shard_map/psum | solution.py:122
  435.7 1.1 multiply_reduce_fusion.1
  436.8 0.6 fusion.96
  437.5 19.5 %all_gather.15 = bf16[512,768]{1,0:T(8,128)(2,1)S(1)} all-gather(bf16[128,768]{1,0:T(8,128)(2,1)S(1)} %fusion.96), channel_id=1, replica_groups=mesh['row'=8,'col'=4] {'col'}, dimensions={0}, use_global_device_ids=true | all-gather | bytes 983040 | tf_op jit(solution)/shard_map/all_gather | solution.py:126
  457.0 0.9 copy.42
  (54 shorter events, 1.4 us)
Async XLA Ops:
  7.2 1.6 copy-start.2
  7.2 97.4 %all-gather.4.cloned.1.call-start = ((), (), s32[]{:S(2)}) async-start(), calls=%async_computation.2 | async-start | bytes 5898240 | tf_op jit(solution)/shard_map/all_gather | solution.py:63
  7.9 4.6 copy-start.7
  7.9 4.8 %copy-start.3 = (bf16[512,768]{1,0:T(8,128)(2,1)S(1)}, bf16[512,768]{1,0:T(8,128)(2,1)}, u32[]{:S(2)}) copy-start(bf16[512,768]{1,0:T(8,128)(2,1)} %param.17) | copy-start | bytes 2359300
  7.9 186.0 %all-gather.6.cloned.1.call-start = ((), (), s32[]{:S(2)}) async-start(), calls=%async_computation.3 | async-start | bytes 5898240 | tf_op jit(solution)/shard_map/all_gather | solution.py:68
  8.7 235.6 %all-gather.8.cloned.1.call-start = ((), (), s32[]{:S(2)}) async-start(), calls=%async_computation.4 | async-start | bytes 2949120 | tf_op jit(solution)/shard_map/all_gather | solution.py:74
  8.8 5.3 %collective-permute-start = (bf16[3,24,768]{2,1,0:T(8,128)(2,1)S(1)}, bf16[3,24,768]{2,1,0:T(8,128)(2,1)S(1)}, u32[]{:S(2)}, u32[]{:S(2)}) collective-permute-start(bf16[3,24,768]{2,1,0:T(8,128)(2,1)S(1)} %get-tuple-element.62), channel_id=1, source_target_pairs={{0,4},{4,8},{8,12},{12,16},{16,20},{20,24},{24,28},{1,5},{5,9},{9,... | collective-permute-start | bytes 331784 | tf_op jit(solution)/shard_map/ppermute | solution.py:19
  11.2 5.3 %collective-permute-start.1 = (bf16[3,24,768]{2,1,0:T(8,128)(2,1)S(1)}, bf16[3,24,768]{2,1,0:T(8,128)(2,1)S(1)}, u32[]{:S(2)}, u32[]{:S(2)}) collective-permute-start(bf16[3,24,768]{2,1,0:T(8,128)(2,1)S(1)} %get-tuple-element.61), channel_id=1, source_target_pairs={{4,0},{8,4},{12,8},{16,12},{20,16},{24,20},{28,24},{5,1},{9,5},{13... | collective-permute-start | bytes 331784 | tf_op jit(solution)/shard_map/ppermute | solution.py:21
  12.5 347.2 %reduce-scatter.3.cloned.1.call-start = ((), (), s32[]{:S(2)}) async-start(), calls=%async_computation.5 | async-start | bytes 1966080 | tf_op jit(solution)/shard_map/reduce_scatter | solution.py:120
  16.6 9.2 %collective-permute-start.2 = (bf16[22,3,768]{2,1,0:T(4,128)(2,1)S(1)}, bf16[22,3,768]{2,1,0:T(4,128)(2,1)S(1)}, u32[]{:S(2)}, u32[]{:S(2)}) collective-permute-start(bf16[22,3,768]{2,1,0:T(4,128)(2,1)S(1)} %get-tuple-element.59), channel_id=1, source_target_pairs={{0,1},{1,2},{2,3},{4,5},{5,6},{6,7},{8,9},{9,10},{10,11},{12,13},{... | collective-permute-start | bytes 304136 | tf_op jit(solution)/shard_map/ppermute | solution.py:19
  20.1 13.1 %collective-permute-start.3 = (bf16[22,3,768]{2,1,0:T(4,128)(2,1)S(1)}, bf16[22,3,768]{2,1,0:T(4,128)(2,1)S(1)}, u32[]{:S(2)}, u32[]{:S(2)}) collective-permute-start(bf16[22,3,768]{2,1,0:T(4,128)(2,1)S(1)} %get-tuple-element.60), channel_id=1, source_target_pairs={{1,0},{2,1},{3,2},{5,4},{6,5},{7,6},{9,8},{10,9},{11,10},{13,12},{... | collective-permute-start | bytes 304136 | tf_op jit(solution)/shard_map/ppermute | solution.py:21
  45.9 0.7 copy-start.8
  45.9 0.7 copy-start.9
  201.9 45.1 %copy-start.11 = (bf16[384,768]{1,0:T(8,128)(2,1)}, bf16[384,768]{1,0:T(8,128)(2,1)S(1)}, u32[]{:S(2)}) copy-start(bf16[384,768]{1,0:T(8,128)(2,1)S(1)} %fusion.34) | copy-start | bytes 1769476
  248.9 1.8 copy-start.4
  248.9 1.8 copy-start.6
  257.5 3.6 copy-start
  261.1 3.0 copy-start.5
  310.0 1.0 copy-start.1
  310.0 70.2 %reduce-scatter.5.cloned.1.call-start = ((), (), s32[]{:S(2)}) async-start(), calls=%async_computation.7 | async-start | bytes 40960 | tf_op jit(solution)/shard_map/reduce_scatter | solution.py:119
  310.9 12.5 %collective-permute-start.4 = (bf16[768,192]{0,1:T(8,128)(2,1)S(1)}, bf16[768,192]{0,1:T(8,128)(2,1)S(1)}, u32[]{:S(2)}, u32[]{:S(2)}) collective-permute-start(bf16[768,192]{0,1:T(8,128)(2,1)S(1)} %copy-done.1), channel_id=1, source_target_pairs={{0,1},{1,2},{2,3},{3,0},{4,5},{5,6},{6,7},{7,4},{8,9},{9,10},{10,1... | collective-permute-start | bytes 884744 | tf_op jit(solution)/shard_map/ppermute | solution.py:79
  323.5 16.2 %collective-permute-start.5 = (bf16[768,192]{0,1:T(8,128)(2,1)S(1)}, bf16[768,192]{0,1:T(8,128)(2,1)S(1)}, u32[]{:S(2)}, u32[]{:S(2)}) collective-permute-start(bf16[768,192]{0,1:T(8,128)(2,1)S(1)} %collective-permute-done.4), channel_id=1, source_target_pairs={{0,1},{1,2},{2,3},{3,0},{4,5},{5,6},{6,7},{7,4},{8,9},{9,10},{10,1... | collective-permute-start | bytes 884744 | tf_op jit(solution)/shard_map/ppermute | solution.py:79
  339.7 18.5 %collective-permute-start.6 = (bf16[768,192]{0,1:T(8,128)(2,1)S(1)}, bf16[768,192]{0,1:T(8,128)(2,1)S(1)}, u32[]{:S(2)}, u32[]{:S(2)}) collective-permute-start(bf16[768,192]{0,1:T(8,128)(2,1)S(1)} %collective-permute-done.5), channel_id=1, source_target_pairs={{0,1},{1,2},{2,3},{3,0},{4,5},{5,6},{6,7},{7,4},{8,9},{9,10},{10,1... | collective-permute-start | bytes 884744 | tf_op jit(solution)/shard_map/ppermute | solution.py:79
  358.4 77.3 %all-reduce.2.cloned.1.call-start = ((), (), s32[]{:S(2)}) async-start(), calls=%async_computation.6 | async-start | bytes 786432 | tf_op jit(solution)/shard_map/psum | solution.py:122
  359.7 77.1 %copy-start.10 = (f32[768]{0:T(1024)S(1)}, f32[768]{0:T(1024)}, u32[]{:S(2)}) copy-start(f32[768]{0:T(1024)} %param.18) | copy-start | bytes 9220
Sparse Core Ops, SparseCore 0:
  9.6 94.9 all-gather.3
  106.1 87.7 all-gather.5
  195.6 48.6 all-gather.7
  310.1 49.5 reduce-scatter.2
  361.8 18.3 reduce-scatter.4
  383.1 52.5 all-reduce.1
